TPU v7x, 512 devices: a whole 4x4x16 slice. The times are simulated.
512 devices in a mesh: expert: 64 (over x, y, z_lo), tensor: 8 (over z_hi, core).
Axes of the slice: x: 4, y: 4, z: 16 (z_hi: 4, z_lo: 4; z = z_hi * 4 + z_lo), core: 2. Of those that a mesh axis runs over, the one named last changes fastest.
Arguments:
- batch_one: bfloat16 [32768, 1536], P(('expert', 'tensor')), may hold values from -6 to 6
- batch_two: bfloat16 [32768, 1536], P(('expert', 'tensor')), may hold values from -6 to 6
- norm_gain: bfloat16 [1536], replicated, may hold values from 0.25 to 1.75
- slots_one: int32 [32768, 8], P(('expert', 'tensor')), may hold values from 0 to 63, all different within a row; in each aligned block of 64 rows (0 to 63, 64 to 127, ...) at most 9 rows name the same one
- slots_two: int32 [32768, 8], P(('expert', 'tensor')), may hold values from 0 to 63, all different within a row; in each aligned block of 64 rows (0 to 63, 64 to 127, ...) at most 9 rows name the same one
- gates_one: float32 [32768, 8], P(('expert', 'tensor')), may hold values from 0.2 to 1
- gates_two: float32 [32768, 8], P(('expert', 'tensor')), may hold values from 0.2 to 1
- table_old: int32 [64], replicated, may hold values from 0 to 39, as said below
- table_new: int32 [64], replicated, may hold values from 0 to 39, as said below
- gate_old: bfloat16 [64, 1536, 512], P('expert', 'tensor'), as said below
- up_old: bfloat16 [64, 1536, 512], P('expert', 'tensor'), as said below
- down_old: bfloat16 [64, 512, 1536], P('expert', None, 'tensor'), as said below
Outputs:
- mixed_one: bfloat16 [32768, 1536], P(('expert', 'tensor'))
- mixed_two: bfloat16 [32768, 1536], P(('expert', 'tensor'))
Inputs may be any that keep to these rules, and one draw needn't show every extreme that they name: `slots_one`: the 8 routes of a token name different slots; among the 64 tokens of one device no slot is named by more than 9 routes, a bound that some block reaches. `slots_two`: the 8 routes of a token name different slots; among the 64 tokens of one device no slot is named by more than 9 routes, a bound that some block reaches. `table_old`: when 64 >= 40 every expert is held by at least one slot; several slots may hold the same expert. table_new[s] equals table_old at slot s, s - 1 or s + 1 (modulo 64), and each of the three cases occurs. `gate_old`: slots that hold the same expert under table_old hold equal weights. `up_old`: slots that hold the same expert under table_old hold equal weights. `down_old`: slots that hold the same expert under table_old hold equal weights.
All inputs are finite; a program needn't handle non-finite values.
Results may differ from a plain program's by a relative error of at most 0.0071.
Values may be sent and summed in bfloat16 or wider, within the bound.
A program may use at most 128 MiB of HBM per device.

v0:
```python
import jax
import jax.numpy as jnp
from jax import lax
from jax.sharding import PartitionSpec as P

EPS = 1e-05


def shifted(block, axis, distance):
    devices = range(lax.axis_size(axis))
    route = [((i - distance) % len(devices), i) for i in devices]
    return lax.ppermute(block, axis, route)


def rms_rows(tokens, norm_gain):
    values = tokens.astype(jnp.float32)
    square = jnp.mean(values * values, axis=-1, keepdims=True)
    return (values * lax.rsqrt(square + EPS) * norm_gain.astype(jnp.float32)).astype(jnp.bfloat16)


def gather_full(shards):
    return (
        lax.all_gather(shards[0], "tensor", axis=0, tiled=True),
        lax.all_gather(shards[1], "tensor", axis=0, tiled=True),
        lax.all_gather(shards[2], "tensor", axis=1, tiled=True),
    )


def expert_block(weights, received):
    gate_full, up_full, down_full = weights
    sources, block_len, features = received.shape
    row_block = received.reshape(sources * block_len, features)
    gate_act = jnp.dot(row_block, gate_full, preferred_element_type=jnp.float32)
    up_act = jnp.dot(row_block, up_full, preferred_element_type=jnp.float32)
    hidden = (jax.nn.silu(gate_act) * up_act).astype(jnp.bfloat16)
    result = jnp.dot(hidden, down_full, preferred_element_type=jnp.float32).astype(jnp.bfloat16)
    result = result.reshape(sources, block_len, features)
    return lax.all_to_all(result, "expert", split_axis=0, concat_axis=0, tiled=True)


def moe_batch(tokens, norm_gain, route_slots, route_gates, weights):
    normed = rms_rows(tokens, norm_gain)
    tok_rows = normed.shape[0]
    top_count = route_slots.shape[1]
    group_size = lax.axis_size("expert")
    capacity = 9 * tok_rows // group_size
    flat_slot = route_slots.reshape(-1)
    onehot = (flat_slot[:, None] == jnp.arange(group_size, dtype=jnp.int32)[None, :]).astype(
        jnp.int32
    )
    running = jnp.cumsum(onehot, axis=0) - 1
    position = jnp.sum(running * onehot, axis=1)
    target = flat_slot * capacity + position
    places = jnp.arange(group_size * capacity, dtype=jnp.int32)
    picker = jnp.any(
        places[:, None, None] == target.reshape(tok_rows, top_count)[None, :, :], axis=2
    ).astype(jnp.bfloat16)
    outgoing = jnp.dot(picker, normed, preferred_element_type=jnp.float32).astype(jnp.bfloat16)
    outgoing = outgoing.reshape(group_size, capacity, normed.shape[1])
    returned = expert_block(
        weights, lax.all_to_all(outgoing, "expert", split_axis=0, concat_axis=0, tiled=True)
    )
    flat_back = returned.reshape(group_size * capacity, normed.shape[1])
    picked = (
        jnp.take(flat_back, target, axis=0)
        .astype(jnp.float32)
        .reshape(tok_rows, top_count, normed.shape[1])
    )
    return jnp.sum(picked * route_gates[:, :, None], axis=1).astype(jnp.bfloat16)


def flatten_all(pieces):
    return jnp.concatenate([piece.reshape(-1) for piece in pieces])


def unflatten(flat, templates):
    pieces = []
    begin = 0
    for template in templates:
        length = template.size
        pieces.append(flat[begin : begin + length].reshape(template.shape))
        begin = begin + length
    return tuple(pieces)


def shard_neighbours(flat):
    found = []
    for offset in (1, -1):
        found.append(shifted(flat, "expert", offset))
    return found


def local(
    batch_one,
    batch_two,
    norm_gain,
    slots_one,
    slots_two,
    gates_one,
    gates_two,
    table_old,
    table_new,
    gate_old,
    up_old,
    down_old,
):
    shards = (gate_old[0], up_old[0], down_old[0])
    full_old = gather_full(shards)
    mixed_one = moe_batch(batch_one, norm_gain, slots_one, gates_one, full_old)
    slot_index = lax.axis_index("expert")
    group = table_old.shape[0]
    wanted = table_new[slot_index]
    keep_own = wanted == table_old[slot_index]
    from_left = wanted == table_old[(slot_index - 1) % group]
    mine = flatten_all(shards)
    beside = shard_neighbours(mine)
    fresh = jnp.where(keep_own, mine, jnp.where(from_left, beside[0], beside[1]))
    full_new = gather_full(unflatten(fresh, shards))
    mixed_two = moe_batch(batch_two, norm_gain, slots_two, gates_two, full_new)
    return (mixed_one, mixed_two)


def solution(mesh):
    in_specs = (
        P(("expert", "tensor"), None),
        P(("expert", "tensor"), None),
        P(),
        P(("expert", "tensor"), None),
        P(("expert", "tensor"), None),
        P(("expert", "tensor"), None),
        P(("expert", "tensor"), None),
        P(),
        P(),
        P("expert", "tensor", None),
        P("expert", "tensor", None),
        P("expert", None, "tensor"),
    )
    out_specs = (P(("expert", "tensor"), None), P(("expert", "tensor"), None))
    return jax.shard_map(local, mesh=mesh, in_specs=in_specs, out_specs=out_specs, check_vma=False)
```

profile of v0, /device:TPU:1, one launch (start us, length us, event | category | flops | bytes accessed | tf_op | source)
XLA Modules:
  0.0 559.8 jit_solution(5104929326630823602)
XLA Ops:
  12.7 4.4 collective-permute-start
  17.1 9.3 %collective-permute-start.1 = (bf16[294912]{0:T(1024)(128)(2,1)}, bf16[294912]{0:T(1024)(128)(2,1)}, u32[]{:S(2)}, u32[]{:S(2)}) collective-permute-start(bf16[294912]{0:T(1024)(128)(2,1)} %constant_dynamic-update-slice_fusion), channel_id=1, source_target_pairs={{8,0},{16,8},{24,16},{32,24},{40,32},{48,40},{56,48},{64,56},{72,6... | collective-permute-start | bytes 1769480 | tf_op jit(solution)/shard_map/ppermute | solution.py:12
  32.3 4.9 all-to-all-start.2
  41.1 5.4 collective-permute-done.1
  59.7 4.2 reshape.146
  63.9 79.0 %all-to-all-done.2 = bf16[64,9,1536]{2,1,0:T(8,128)(2,1)S(1)} async-done(((bf16[64,9,1536]{2,1,0:T(8,128)(2,1)}), bf16[64,9,1536]{2,1,0:T(8,128)(2,1)S(1)}, u32[]{:S(2)}, u32[]{:S(2)}) %all-to-all-start.2) | async-done | bytes 1769504 | tf_op jit(solution)/shard_map/all_to_all | solution.py:61
  142.9 6.9 %all-to-all-start = ((bf16[64,9,1536]{2,1,0:T(8,128)(2,1)}), bf16[64,9,1536]{2,1,0:T(8,128)(2,1)}, u32[]{:S(2)}, u32[]{:S(2)}) async-start(bf16[64,9,1536]{2,1,0:T(8,128)(2,1)} %reshape.146), calls=%async_computation | async-start | bytes 6291456 | tf_op jit(solution)/shard_map/all_to_all | solution.py:61
  153.4 4.2 fusion.42
  157.6 25.5 %all-gather.14.cloned.1.call-done = bf16[512,1536]{0,1:T(8,128)(2,1)} async-done(((bf16[512,192]{0,1:T(8,128)(2,1)}), bf16[512,1536]{0,1:T(8,128)(2,1)}) %all-gather.14.cloned.1.call-update) | async-done | bytes 1572880 | tf_op jit(solution)/shard_map/all_gather | solution.py:25
  183.1 69.2 %all-gather.12.cloned.1.call-done = bf16[1536,512]{1,0:T(8,128)(2,1)} async-done(((bf16[192,512]{1,0:T(8,128)(2,1)}), bf16[1536,512]{1,0:T(8,128)(2,1)}) %all-gather.12.cloned.1.call-update) | async-done | bytes 1572880 | tf_op jit(solution)/shard_map/all_gather | solution.py:24
  252.3 4.3 convolution_convert_fusion.2
  259.1 14.4 %all-to-all-done = bf16[64,9,1536]{2,1,0:T(8,128)(2,1)} async-done(((bf16[64,9,1536]{2,1,0:T(8,128)(2,1)}), bf16[64,9,1536]{2,1,0:T(8,128)(2,1)}, u32[]{:S(2)}, u32[]{:S(2)}) %all-to-all-start) | async-done | bytes 1769504 | tf_op jit(solution)/shard_map/all_to_all | solution.py:61
  273.5 8.8 %all-to-all-start.3 = ((bf16[64,9,1536]{2,1,0:T(8,128)(2,1)}), bf16[64,9,1536]{2,1,0:T(8,128)(2,1)S(1)}, u32[]{:S(2)}, u32[]{:S(2)}) async-start(bf16[64,9,1536]{2,1,0:T(8,128)(2,1)} %reshape.155), calls=%async_computation.3 | async-start | bytes 6291456 | tf_op jit(solution)/shard_map/all_to_all | solution.py:38
  283.5 4.2 reshape.147
  287.7 31.6 %all-gather.16.cloned.1.call-done = bf16[1,1536,512]{2,1,0:T(8,128)(2,1)} async-done(((bf16[1,192,512]{2,1,0:T(8,128)(2,1)}), bf16[1,1536,512]{2,1,0:T(8,128)(2,1)}) %all-gather.16.cloned.1.call-update) | async-done | bytes 1572880 | tf_op jit(solution)/shard_map/all_gather | solution.py:23
  319.3 4.0 fusion.5
  323.3 61.1 %all-gather.18.cloned.1.call-done = bf16[1,1536,512]{2,1,0:T(8,128)(2,1)} async-done(((bf16[1,192,512]{2,1,0:T(8,128)(2,1)}), bf16[1,1536,512]{2,1,0:T(8,128)(2,1)}) %all-gather.18.cloned.1.call-update) | async-done | bytes 1572880 | tf_op jit(solution)/shard_map/all_gather | solution.py:24
  384.5 65.4 %all-gather.20.cloned.1.call-done = bf16[1,512,1536]{1,2,0:T(8,128)(2,1)} async-done(((bf16[1,512,192]{1,2,0:T(8,128)(2,1)}), bf16[1,512,1536]{1,2,0:T(8,128)(2,1)}) %all-gather.20.cloned.1.call-update) | async-done | bytes 1572880 | tf_op jit(solution)/shard_map/all_gather | solution.py:25
  449.8 6.0 %convolution_convert_fusion.3 = bf16[576,1536]{1,0:T(8,128)(2,1)} fusion(bf16[1,512,1536]{1,2,0:T(8,128)(2,1)} %all-gather.20.cloned.1.call-done, bf16[576,1536]{1,0:T(8,128)(2,1)} %reshape.147, bf16[1,1536,512]{2,1,0:T(8,128)(2,1)} %all-gather.18.cloned.1.call-done, f32[576,512]{1,0:T(8,128)} %fusion.5), kind=kOutput, calls=%fused_computation.9 | convolution fusion | flops 1814593536 | bytes 7864320 | tf_op jit(solution)/shard_map/dot_general | solution.py:36
  455.9 4.2 reshape.148
  461.8 8.2 %all-to-all-start.1 = ((bf16[64,9,1536]{2,1,0:T(8,128)(2,1)}), bf16[64,9,1536]{2,1,0:T(8,128)(2,1)}, u32[]{:S(2)}, u32[]{:S(2)}) async-start(bf16[64,9,1536]{2,1,0:T(8,128)(2,1)} %reshape.148), calls=%async_computation.1 | async-start | bytes 6291456 | tf_op jit(solution)/shard_map/all_to_all | solution.py:38
  470.3 3.0 reshape.156
  475.4 67.4 %all-to-all-done.1 = bf16[64,9,1536]{2,1,0:T(8,128)(2,1)} async-done(((bf16[64,9,1536]{2,1,0:T(8,128)(2,1)}), bf16[64,9,1536]{2,1,0:T(8,128)(2,1)}, u32[]{:S(2)}, u32[]{:S(2)}) %all-to-all-start.1) | async-done | bytes 1769504 | tf_op jit(solution)/shard_map/all_to_all | solution.py:38
  542.8 3.0 reshape.149
  (104 shorter events, 44.3 us)
Async XLA Ops:
  7.2 19.2 %copy-start.6 = (s32[64,8]{0,1:T(8,128)S(1)}, s32[64,8]{0,1:T(8,128)}, u32[]{:S(2)}) copy-start(s32[64,8]{0,1:T(8,128)} %param.18) | copy-start | bytes 6148
  8.9 20.1 %copy-start.8 = (bf16[1536]{0:T(1024)(128)(2,1)S(1)}, bf16[1536]{0:T(1024)(128)(2,1)}, u32[]{:S(2)}) copy-start(bf16[1536]{0:T(1024)(128)(2,1)} %param.16) | copy-start | bytes 9220
  8.9 20.2 %copy-start.3 = (bf16[64,1536]{1,0:T(8,128)(2,1)S(1)}, bf16[64,1536]{1,0:T(8,128)(2,1)}, u32[]{:S(2)}) copy-start(bf16[64,1536]{1,0:T(8,128)(2,1)} %param.15) | copy-start | bytes 589828
  12.7 28.4 %collective-permute-start = (bf16[294912]{0:T(1024)(128)(2,1)}, bf16[294912]{0:T(1024)(128)(2,1)}, u32[]{:S(2)}, u32[]{:S(2)}) collective-permute-start(bf16[294912]{0:T(1024)(128)(2,1)} %constant_dynamic-update-slice_fusion), channel_id=1, source_target_pairs={{504,0},{0,8},{8,16},{16,24},{24,32},{32,40},{40,48},{48,56},{56,6... | collective-permute-start | bytes 1769480 | tf_op jit(solution)/shard_map/ppermute | solution.py:12
  17.1 29.4 %collective-permute-start.1 = (bf16[294912]{0:T(1024)(128)(2,1)}, bf16[294912]{0:T(1024)(128)(2,1)}, u32[]{:S(2)}, u32[]{:S(2)}) collective-permute-start(bf16[294912]{0:T(1024)(128)(2,1)} %constant_dynamic-update-slice_fusion), channel_id=1, source_target_pairs={{8,0},{16,8},{24,16},{32,24},{40,32},{48,40},{56,48},{64,56},{72,6... | collective-permute-start | bytes 1769480 | tf_op jit(solution)/shard_map/ppermute | solution.py:12
  32.3 5.0 copy-start.12
  32.3 5.6 copy-start.11
  32.3 110.5 %all-to-all-start.2 = ((bf16[64,9,1536]{2,1,0:T(8,128)(2,1)}), bf16[64,9,1536]{2,1,0:T(8,128)(2,1)S(1)}, u32[]{:S(2)}, u32[]{:S(2)}) async-start(bf16[64,9,1536]{2,1,0:T(8,128)(2,1)} %reshape.153), calls=%async_computation.2 | async-start | bytes 6291456 | tf_op jit(solution)/shard_map/all_to_all | solution.py:61
  37.2 116.2 %all-gather.10.cloned.1.call-start = ((), (), s32[]{:S(2)}) async-start(), calls=%async_computation.4 | async-start | bytes 1769472 | tf_op jit(solution)/shard_map/all_gather | solution.py:23
  46.5 3.8 copy-start.7
  47.6 6.7 %copy-start.4 = (bf16[64,1536]{1,0:T(8,128)(2,1)S(1)}, bf16[64,1536]{1,0:T(8,128)(2,1)}, u32[]{:S(2)}) copy-start(bf16[64,1536]{1,0:T(8,128)(2,1)} %param.14) | copy-start | bytes 589828
  50.2 132.9 %all-gather.14.cloned.1.call-start = ((), (), s32[]{:S(2)}) async-start(), calls=%async_computation.6 | async-start | bytes 1769472 | tf_op jit(solution)/shard_map/all_gather | solution.py:25
  63.9 85.9 %copy-start.5 = (bf16[98304]{0:T(1024)(128)(2,1)S(1)}, bf16[98304]{0:T(1024)(128)(2,1)}, u32[]{:S(2)}) copy-start(bf16[98304]{0:T(1024)(128)(2,1)} %get-tuple-element.9) | copy-start | bytes 589828
  142.9 130.6 %all-to-all-start = ((bf16[64,9,1536]{2,1,0:T(8,128)(2,1)}), bf16[64,9,1536]{2,1,0:T(8,128)(2,1)}, u32[]{:S(2)}, u32[]{:S(2)}) async-start(bf16[64,9,1536]{2,1,0:T(8,128)(2,1)} %reshape.146), calls=%async_computation | async-start | bytes 6291456 | tf_op jit(solution)/shard_map/all_to_all | solution.py:61
  149.8 102.5 %all-gather.12.cloned.1.call-start = ((), (), s32[]{:S(2)}) async-start(), calls=%async_computation.5 | async-start | bytes 1769472 | tf_op jit(solution)/shard_map/all_gather | solution.py:24
  150.7 168.6 %all-gather.16.cloned.1.call-start = ((), (), s32[]{:S(2)}) async-start(), calls=%async_computation.7 | async-start | bytes 1769472 | tf_op jit(solution)/shard_map/all_gather | solution.py:23
  153.4 98.9 %copy-start.2 = (bf16[576,1536]{1,0:T(8,128)(2,1)S(1)}, bf16[576,1536]{1,0:T(8,128)(2,1)}, u32[]{:S(2)}) copy-start(bf16[576,1536]{1,0:T(8,128)(2,1)} %reshape.154) | copy-start | bytes 5308420
  273.5 186.6 %all-to-all-start.3 = ((bf16[64,9,1536]{2,1,0:T(8,128)(2,1)}), bf16[64,9,1536]{2,1,0:T(8,128)(2,1)S(1)}, u32[]{:S(2)}, u32[]{:S(2)}) async-start(bf16[64,9,1536]{2,1,0:T(8,128)(2,1)} %reshape.155), calls=%async_computation.3 | async-start | bytes 6291456 | tf_op jit(solution)/shard_map/all_to_all | solution.py:38
  282.3 102.1 %all-gather.18.cloned.1.call-start = ((), (), s32[]{:S(2)}) async-start(), calls=%async_computation.8 | async-start | bytes 1769472 | tf_op jit(solution)/shard_map/all_gather | solution.py:24
  282.9 166.9 %all-gather.20.cloned.1.call-start = ((), (), s32[]{:S(2)}) async-start(), calls=%async_computation.9 | async-start | bytes 1769472 | tf_op jit(solution)/shard_map/all_gather | solution.py:25
  460.1 10.0 %copy-start.9 = (f32[64,8]{0,1:T(8,128)S(1)}, f32[64,8]{0,1:T(8,128)}, u32[]{:S(2)}) copy-start(f32[64,8]{0,1:T(8,128)} %param.20) | copy-start | bytes 6148
  460.1 10.0 %copy-start.10 = (f32[64,8]{0,1:T(8,128)S(1)}, f32[64,8]{0,1:T(8,128)}, u32[]{:S(2)}) copy-start(f32[64,8]{0,1:T(8,128)} %param.19) | copy-start | bytes 6148
  461.8 81.1 %all-to-all-start.1 = ((bf16[64,9,1536]{2,1,0:T(8,128)(2,1)}), bf16[64,9,1536]{2,1,0:T(8,128)(2,1)}, u32[]{:S(2)}, u32[]{:S(2)}) async-start(bf16[64,9,1536]{2,1,0:T(8,128)(2,1)} %reshape.148), calls=%async_computation.1 | async-start | bytes 6291456 | tf_op jit(solution)/shard_map/all_to_all | solution.py:38
  548.8 2.1 copy-start.1
  (1 other events, 1.7 us)
Sparse Core Ops, SparseCore 0:
  50.4 65.8 all-gather.9
  118.9 64.1 all-gather.13
  185.8 66.4 all-gather.11
  254.3 64.9 all-gather.15
  321.2 63.1 all-gather.17
  386.4 63.3 all-gather.19
where the time goes:
time: 561 us; the launch traced here: 560 us
  waiting for transfers between devices  420 us (75%)
  local copies, waits for them, and re-layouts  46.2 us (8%)
  starting transfers between devices  42.9 us (8%)
  matrix products  22.1 us (4%)
  between operations  17 us (3%)
  other arithmetic  11.3 us (2%)
    all_gather x2, waiting for transfers between devices, gather_full(): lax.all_gather(shards[1], 'tensor', axis=0, tiled=True)  130 us
    all_to_all x2, waiting for transfers between devices, moe_batch(): lax.all_to_all(outgoing, 'expert', split_axis=0, concat_axis=0, tiled=True)  93.3 us
    all_gather x2, waiting for transfers between devices, gather_full(): lax.all_gather(shards[2], 'tensor', axis=1, tiled=True)  90.9 us
    all_to_all x2, waiting for transfers between devices, expert_block(): lax.all_to_all(result, 'expert', split_axis=0, concat_axis=0, tiled=True)  67.5 us
    all_gather x2, waiting for transfers between devices, gather_full(): lax.all_gather(shards[0], 'tensor', axis=0, tiled=True)  31.6 us
    all_to_all x2, starting transfers between devices, expert_block(): lax.all_to_all(result, 'expert', split_axis=0, concat_axis=0, tiled=True)  17.1 us
    ppermute x2, starting transfers between devices, shifted(): return lax.ppermute(block, axis, route)  13.6 us
    all_to_all x2, starting transfers between devices, moe_batch(): lax.all_to_all(outgoing, 'expert', split_axis=0, concat_axis=0, tiled=True)  11.7 us
  transfers between devices with their start and end apart: 12, of which 9 were waited for; matrix products, arithmetic and copies ran while one was open for 11% of the time, Pallas kernels for 0%

commit v1 on v0

v1 whole, which is shorter than its diff:
```python
import functools

import jax
import jax.numpy as jnp
from jax import lax
from jax.experimental import pallas as pl
from jax.experimental.pallas import tpu as pltpu
from jax.sharding import PartitionSpec as P

EPS = 1e-05
MESH = pl.DeviceIdType.MESH
BF16 = jnp.bfloat16
F32 = jnp.float32

LINE = 4
PLANE = 16
HIGH = 4
ROWS = 40
PAD = 48
GROUP = 4


def body(
    x1, x2, gain, r1, r2, told, tnew, gate_in, up_in, down_in,
    o1, o2,
    wg, wu, wd, xg, rg, outg, recv, res, back, pick, part, precv, tgt, gat,
    ring_s, ring_r, far_s, far_r, sib_s, sib_r, nbr_s, nbr_r,
    zx_s, zx_r, zr_s, zr_r, a_s, a_r, a_l, b_s, b_r, b_l, p_s, p_r,
):
    e = lax.axis_index("expert")
    t = lax.axis_index("tensor")
    experts = lax.axis_size("expert")
    tensors = lax.axis_size("tensor")
    zl = e % LINE
    p = e // LINE
    zh = t // 2
    c = t % 2
    right = (e, (t + 2) % tensors)
    left = (e, (t + tensors - 2) % tensors)
    sibling = (e, zh * 2 + (1 - c))
    up_hop = (zl + 1) // LINE
    down_hop = 1 - (zl + LINE - 1) // LINE
    after = ((e + 1) % experts, (t + 2 * up_hop) % tensors)
    before = ((e + experts - 1) % experts, (t + tensors - 2 * down_hop) % tensors)
    weights = (wg, wu, wd)
    tokens, features = x1.shape

    def remote(src, dst, ss, rs, device):
        return pltpu.make_async_remote_copy(
            src_ref=src, dst_ref=dst, send_sem=ss, recv_sem=rs,
            device_id=device, device_id_type=MESH,
        )

    blank = jnp.zeros((PLANE, 16, features), BF16)
    for b in range(2):
        recv[b, :, PAD - 16:PAD, :] = blank
        back[b, :, PAD - 16:PAD, :] = blank

    barrier = pltpu.get_barrier_semaphore()

    def greet(device):
        pl.semaphore_signal(barrier, inc=1, device_id=device, device_id_type=MESH)

    for device in (right, left, sibling, after, before):
        greet(device)
    for o in range(1, LINE):
        greet((p * LINE + (zl + o) % LINE, t))

    def greet_plane(o, carry):
        greet((((p + o) % PLANE) * LINE + zl, t))
        return carry

    lax.fori_loop(1, PLANE, greet_plane, 0)
    pl.semaphore_wait(barrier, 5 + LINE - 1 + PLANE - 1)

    for w, shard in zip(weights, (gate_in, up_in, down_in)):
        w[0, zh, c] = shard[...]

    def ring(m, way):
        w = weights[m]
        return remote(
            w.at[0, zh, c], w.at[0, zh, c], ring_s.at[m, way], ring_r.at[m, way],
            (right, left)[way],
        )

    def far(m, way):
        w = weights[m]
        owner = (zh + HIGH - 1) % HIGH if way == 0 else (zh + 1) % HIGH
        half = pl.ds(way * (w.shape[3] // 2), w.shape[3] // 2)
        place = w.at[0, owner, c, half]
        return remote(place, place, far_s.at[m, way], far_r.at[m, way], (right, left)[way])

    def sib(v, m):
        w = weights[m]
        place = w.at[v, :, c]
        return remote(place, place, sib_s.at[v, m], sib_r.at[v, m], sibling)

    def nbr(m, way):
        w = weights[m]
        return remote(
            w.at[0, :, c], w.at[1 + way, :, c], nbr_s.at[m, way], nbr_r.at[m, way],
            (after, before)[way],
        )

    for m in range(3):
        for way in range(2):
            ring(m, way).start()

    def line_x(b, o):
        return remote(
            xg.at[b, zl], xg.at[b, zl], zx_s.at[b, o], zx_r.at[b, zl],
            (p * LINE + (zl + o) % LINE, t),
        )

    def line_r(b, o):
        return remote(
            rg.at[b, zl], rg.at[b, zl], zr_s.at[b, o], zr_r.at[b, zl],
            (p * LINE + (zl + o) % LINE, t),
        )

    def line_x_in(b, o):
        i = (zl + o) % LINE
        return remote(xg.at[b, i], xg.at[b, i], zx_s.at[b, o], zx_r.at[b, i], (p * LINE + i, t))

    def line_r_in(b, o):
        i = (zl + o) % LINE
        return remote(rg.at[b, i], rg.at[b, i], zr_s.at[b, o], zr_r.at[b, i], (p * LINE + i, t))

    scale = gain[...].astype(F32)
    for b, (x, r) in enumerate(((x1, r1), (x2, r2))):
        values = x[...].astype(F32)
        square = jnp.mean(values * values, axis=-1, keepdims=True)
        xg[b, zl] = (values * lax.rsqrt(square + EPS) * scale).astype(BF16)
        rg[b, zl] = r[...]
        for o in range(1, LINE):
            line_x(b, o).start()
            line_r(b, o).start()

    def block_send(b, d, src, dst, ss, rs, ls):
        @pl.when(d != p)
        def _():
            remote(
                src.at[b, d, pl.ds(0, ROWS)], dst.at[b, p, pl.ds(0, ROWS)],
                ss.at[b, d], rs.at[b, p], (d * LINE + zl, t),
            ).start()

        @pl.when(d == p)
        def _():
            pltpu.make_async_copy(
                src.at[b, d, pl.ds(0, ROWS)], dst.at[b, p, pl.ds(0, ROWS)], ls.at[b]
            ).start()

    def block_wait(b, src, dst, ss, rs, ls, which):
        def one(o, carry):
            d = (p + o) % PLANE
            copy = remote(
                src.at[b, d, pl.ds(0, ROWS)], dst.at[b, d, pl.ds(0, ROWS)],
                ss.at[b, d], rs.at[b, d], (d * LINE + zl, t),
            )
            if which == "in":
                copy.wait_recv()
            else:
                copy.wait_send()
            return carry

        lax.fori_loop(1, PLANE, one, 0)
        if which == "in":
            pltpu.make_async_copy(
                src.at[b, p, pl.ds(0, ROWS)], dst.at[b, p, pl.ds(0, ROWS)], ls.at[b]
            ).wait()

    def route(b):
        ids = (lax.broadcasted_iota(jnp.int32, (PLANE, tokens), 0) * LINE + zl).astype(F32)
        first = lax.broadcasted_iota(jnp.int32, (tokens, tokens), 0)
        second = lax.broadcasted_iota(jnp.int32, (tokens, tokens), 1)
        ahead = jnp.where(first < second, 1.0, 0.0).astype(BF16)
        targets, gates = [], []
        for i in range(LINE):
            info = rg[b, i]
            named = jnp.zeros((PLANE, tokens), F32)
            gate = jnp.zeros((PLANE, tokens), F32)
            for k in range(8):
                same = info[k:k + 1, :] == ids
                named = named + jnp.where(same, 1.0, 0.0)
                gate = gate + jnp.where(same, info[8 + k:9 + k, :], 0.0)
            rank = jnp.dot(named.astype(BF16), ahead, preferred_element_type=F32)
            targets.append(jnp.where(named > 0.5, rank * LINE + i, -1.0))
            gates.append(gate)
        tgt[b] = jnp.concatenate(targets, axis=1)
        gat[b] = jnp.concatenate(gates, axis=1)

    places = lax.broadcasted_iota(jnp.int32, (PAD, LINE * tokens), 0).astype(F32)

    def dispatch(b):
        route(b)
        for d in range(PLANE):
            pick[d] = jnp.where(tgt[b, d:d + 1, :] == places, 1.0, 0.0).astype(BF16)

        def group(q, carry):
            rows = pick[pl.ds(q * GROUP, GROUP)].reshape(GROUP * PAD, LINE * tokens)
            block = jnp.dot(
                rows, xg[b].reshape(LINE * tokens, features), preferred_element_type=F32
            ).astype(BF16)
            outg[b, pl.ds(q * GROUP, GROUP)] = block.reshape(GROUP, PAD, features)
            for j in range(GROUP):
                block_send(b, q * GROUP + j, outg, recv, a_s, a_r, a_l)
            return carry

        lax.fori_loop(0, PLANE // GROUP, group, 0)

    for b in range(2):
        for o in range(1, LINE):
            line_x_in(b, o).wait_recv()
            line_r_in(b, o).wait_recv()
        dispatch(b)

    def ring_in(m, way):
        w = weights[m]
        owner = (zh + HIGH - 1) % HIGH if way == 0 else (zh + 1) % HIGH
        place = w.at[0, owner, c]
        return remote(place, place, ring_s.at[m, way], ring_r.at[m, way], (right, left)[way])

    def far_in(m, way):
        w = weights[m]
        half = pl.ds(way * (w.shape[3] // 2), w.shape[3] // 2)
        place = w.at[0, (zh + 2) % HIGH, c, half]
        return remote(place, place, far_s.at[m, way], far_r.at[m, way], (right, left)[way])

    def sib_in(v, m):
        w = weights[m]
        place = w.at[v, :, 1 - c]
        return remote(place, place, sib_s.at[v, m], sib_r.at[v, m], sibling)

    def nbr_in(m, way):
        w = weights[m]
        place = w.at[1 + way, :, c]
        return remote(place, place, nbr_s.at[m, way], nbr_r.at[m, way], (after, before)[way])

    for m in range(3):
        for way in range(2):
            ring_in(m, way).wait_recv()
            far(m, way).start()
    for m in range(3):
        for way in range(2):
            far_in(m, way).wait_recv()
        sib(0, m).start()
    for m in range(3):
        for way in range(2):
            nbr(m, way).start()
    for m in range(3):
        sib_in(0, m).wait_recv()

    def experts_on(b, v):
        inner = wg.shape[4]

        def group(q, carry):
            rows = recv[b, pl.ds(q * GROUP, GROUP)].reshape(GROUP * PAD, features)
            gate_act = jnp.dot(rows, wg[v].reshape(features, inner), preferred_element_type=F32)
            up_act = jnp.dot(rows, wu[v].reshape(features, inner), preferred_element_type=F32)
            hidden = (gate_act / (1.0 + jnp.exp(-gate_act)) * up_act).astype(BF16)
            result = lax.dot_general(
                hidden, wd[v].reshape(features, inner), (((1,), (1,)), ((), ())),
                preferred_element_type=F32,
            ).astype(BF16)
            res[b, pl.ds(q * GROUP, GROUP)] = result.reshape(GROUP, PAD, features)
            for j in range(GROUP):
                block_send(b, q * GROUP + j, res, back, b_s, b_r, b_l)
            return carry

        lax.fori_loop(0, PLANE // GROUP, group, 0)

    def part_out(b, o):
        i = (zl + o) % LINE
        return remote(
            part.at[b, i], precv.at[b, zl], p_s.at[b, o], p_r.at[b, zl], (p * LINE + i, t)
        )

    def part_in(b, o):
        i = (zl + o) % LINE
        return remote(
            part.at[b, i], precv.at[b, i], p_s.at[b, o], p_r.at[b, i], (p * LINE + i, t)
        )

    def combine(b):
        for d in range(PLANE):
            pick[d] = jnp.where(
                tgt[b, d:d + 1, :] == places, gat[b, d:d + 1, :], 0.0
            ).astype(BF16)
        mixer = pick[...].reshape(PLANE * PAD, LINE * tokens)
        total = lax.dot_general(
            mixer, back[b].reshape(PLANE * PAD, features), (((0,), (0,)), ((), ())),
            preferred_element_type=F32,
        ).astype(BF16)
        part[b] = total.reshape(LINE, tokens, features)
        for o in range(1, LINE):
            part_out(b, o).start()
        precv[b, zl] = part[b, zl]

    def finish(b, out):
        for o in range(1, LINE):
            part_in(b, o).wait_recv()
        total = precv[b, 0].astype(F32)
        for i in range(1, LINE):
            total = total + precv[b, i].astype(F32)
        out[...] = total.astype(BF16)

    block_wait(0, outg, recv, a_s, a_r, a_l, "in")
    experts_on(0, 0)
    block_wait(0, res, back, b_s, b_r, b_l, "in")
    combine(0)

    for m in range(3):
        for way in range(2):
            nbr_in(m, way).wait_recv()
            sib(1 + way, m).start()
    block_wait(1, outg, recv, a_s, a_r, a_l, "in")
    finish(0, o1)
    for m in range(3):
        for way in range(2):
            sib_in(1 + way, m).wait_recv()

    wanted = tnew[e]
    keeps = wanted == told[e]
    lower = wanted == told[(e + experts - 1) % experts]
    experts_on(1, jnp.where(keeps, 0, jnp.where(lower, 1, 2)))
    block_wait(1, res, back, b_s, b_r, b_l, "in")
    combine(1)
    finish(1, o2)

    for m in range(3):
        for way in range(2):
            ring(m, way).wait_send()
            far(m, way).wait_send()
            nbr(m, way).wait_send()
        for v in range(3):
            sib(v, m).wait_send()
    for b in range(2):
        for o in range(1, LINE):
            line_x(b, o).wait_send()
            line_r(b, o).wait_send()
            part_out(b, o).wait_send()
        block_wait(b, outg, recv, a_s, a_r, a_l, "out")
        block_wait(b, res, back, b_s, b_r, b_l, "out")


def local(
    batch_one, batch_two, norm_gain, slots_one, slots_two, gates_one, gates_two,
    table_old, table_new, gate_old, up_old, down_old,
):
    tokens, features = batch_one.shape
    shard, inner = gate_old.shape[1:]
    info = [
        jnp.concatenate([slots.astype(F32).T, gates.T], axis=0)
        for slots, gates in ((slots_one, gates_one), (slots_two, gates_two))
    ]
    vmem = pl.BlockSpec(memory_space=pltpu.VMEM)
    smem = pl.BlockSpec(memory_space=pltpu.SMEM)
    dma = pltpu.SemaphoreType.DMA
    full = pltpu.VMEM((3, HIGH, 2, shard, inner), BF16)
    blocks = pltpu.VMEM((2, PLANE, PAD, features), BF16)
    line = pltpu.VMEM((2, LINE, tokens, features), BF16)
    return pl.pallas_call(
        body,
        out_shape=[jax.ShapeDtypeStruct((tokens, features), BF16)] * 2,
        in_specs=[vmem] * 5 + [smem] * 2 + [vmem] * 3,
        out_specs=[vmem] * 2,
        scratch_shapes=[
            full, full, full,
            line, pltpu.VMEM((2, LINE, 16, tokens), F32),
            blocks, blocks, blocks, blocks,
            pltpu.VMEM((PLANE, PAD, LINE * tokens), BF16),
            line, line,
            pltpu.VMEM((2, PLANE, LINE * tokens), F32), pltpu.VMEM((2, PLANE, LINE * tokens), F32),
            dma((3, 2)), dma((3, 2)), dma((3, 2)), dma((3, 2)),
            dma((3, 3)), dma((3, 3)), dma((3, 2)), dma((3, 2)),
            dma((2, LINE)), dma((2, LINE)), dma((2, LINE)), dma((2, LINE)),
            dma((2, PLANE)), dma((2, PLANE)), dma((2,)),
            dma((2, PLANE)), dma((2, PLANE)), dma((2,)),
            dma((2, LINE)), dma((2, LINE)),
        ],
        compiler_params=pltpu.CompilerParams(
            collective_id=0, has_side_effects=True, vmem_limit_bytes=60 * 1024 * 1024
        ),
    )(
        batch_one, batch_two, norm_gain.reshape(1, features), info[0], info[1],
        table_old, table_new, gate_old[0], up_old[0], down_old[0].T,
    )


def solution(mesh):
    rows = P(("expert", "tensor"), None)
    in_specs = (
        rows, rows, P(), rows, rows, rows, rows, P(), P(),
        P("expert", "tensor", None), P("expert", "tensor", None), P("expert", None, "tensor"),
    )
    return jax.shard_map(
        local, mesh=mesh, in_specs=in_specs, out_specs=(rows, rows), check_vma=False
    )
```

time: 561 us -> 286 us (0.51)
  the two profiles are of different devices: /device:TPU:1 before, /device:TPU:63 now
where the time goes in v1:
time: 286 us
  Pallas kernels  280 us (98%)
  local copies, waits for them, and re-layouts  5.09 us (2%)
    pallas_call x1, Pallas kernels, local(): pl.pallas_call(body, out_shape=[jax.ShapeDtypeStruct((tokens, features),...  280 us

profile of v1, /device:TPU:63, one launch (start us, length us, event | category | flops | bytes accessed | tf_op | source)
XLA Modules:
  0.0 286.1 jit_solution(16991839940238100042)
XLA Ops:
  0.6 0.0 copy-start.1
  0.6 0.7 copy-done.1
  1.3 0.0 copy-start.2
  1.3 0.7 copy-done.2
  2.0 0.0 copy-start.3
  2.0 0.7 copy-done.3
  2.7 0.0 copy-start.4
  2.7 0.0 copy-start.5
  2.7 0.6 reshape.7.gain
  3.3 0.1 copy-done.4
  3.4 0.0 copy-done.5
  3.4 0.6 pad_maximum_fusion
  4.0 279.8 %shard_map.131 = (bf16[64,1536]{1,0:T(8,128)(2,1)}, bf16[64,1536]{1,0:T(8,128)(2,1)}) custom-call(bf16[64,1536]{1,0:T(8,128)(2,1)} %x1.1, bf16[64,1536]{1,0:T(8,128)(2,1)} %x2.1, bf16[1,1536]{1,0:T(2,128)(2,1)} %reshape.7.gain, f32[16,64]{1,0:T(8,128)} %get-tuple-element.2.r1, f32[16,64]{1,0:T(8,128)} %get-tuple-element.3.r2, s32[64]{0:T(128)} %told.1, ...), custom_call_target="tpu_custom_call" | custom-call | tf_op jit(solution)/shard_map/pallas_call | solution.py:362
  283.8 0.0 copy-start
  283.8 1.7 copy.16
  285.5 0.0 copy-done
  285.5 0.7 copy.17
  (2 shorter events, 0.0 us)
Async XLA Ops:
  0.6 0.7 copy-start.1
  1.3 0.7 copy-start.2
  2.0 0.7 copy-start.3
  2.7 0.7 copy-start.4
  2.7 0.7 copy-start.5
  283.8 1.7 copy-start

commit v2 on v1

v2 whole, which is shorter than its diff:
```python
import functools

import jax
import jax.numpy as jnp
from jax import lax
from jax.experimental import pallas as pl
from jax.experimental.pallas import tpu as pltpu
from jax.sharding import PartitionSpec as P

EPS = 1e-05
MESH = pl.DeviceIdType.MESH
BF16 = jnp.bfloat16
F32 = jnp.float32

LINE = 4
DEPTH = 16
PLANE = 16
HIGH = 4
WIDE = 4
ROWS = 40
PAD = 48
HOPS = 11
WHOLE = 4
SHARED = (1, 3, 4, 5, 7, 8, 9, 11)
ORDER = (2, 1, 3, 0)


def body(
    x1, x2, gain, r1, r2, told, tnew, gate_in, up_in, down_in,
    o1, o2,
    wg, wu, wd, xg, rg, outg, recv, res, back, pick, part, precv, tgt, gat,
    ring_s, ring_r, own_s, own_r, sib_s, sib_r, edge_s, edge_r, esib_s, esib_r,
    zx_s, zx_r, zr_s, zr_r, a_s, a_r, a_l, b_s, b_r, b_l, p_s, p_r,
):
    e = lax.axis_index("expert")
    t = lax.axis_index("tensor")
    experts = lax.axis_size("expert")
    zl = e % HIGH
    p = e // HIGH
    px = p // WIDE
    py = p % WIDE
    zh = t // 2
    c = t % 2
    z = zh * HIGH + zl
    top = (zl + 1) // HIGH
    on_edge = zl % (HIGH - 1) == 0
    skip = 2 * (1 - 2 * (z % 2))
    sibling = (e, zh * 2 + (1 - c))
    weights = (wg, wu, wd)
    tokens, features = x1.shape
    shard, inner = gate_in.shape

    def along(distance):
        other = (z + distance + 2 * DEPTH) % DEPTH
        return (p * HIGH + other % HIGH, (other // HIGH) * 2 + c)

    def remote(src, dst, ss, rs, device):
        return pltpu.make_async_remote_copy(
            src_ref=src, dst_ref=dst, send_sem=ss, recv_sem=rs,
            device_id=device, device_id_type=MESH,
        )

    blank = jnp.zeros((PLANE, 16, features), BF16)
    for b in range(2):
        recv[b, :, PAD - 16:PAD, :] = blank
        back[b, :, PAD - 16:PAD, :] = blank

    barrier = pltpu.get_barrier_semaphore()

    def greet(device):
        pl.semaphore_signal(barrier, inc=1, device_id=device, device_id_type=MESH)

    for device in (along(1), along(-1), along(2), along(-2), sibling):
        greet(device)

    def greet_plane(o, carry):
        greet((((p + o) % PLANE) * HIGH + zl, t))
        return carry

    lax.fori_loop(1, PLANE, greet_plane, 0)
    pl.semaphore_wait(barrier, 5 + PLANE - 1)

    def spot(m, column, owner, hop, way):
        place = weights[m].at[column, owner // HIGH, c]
        if hop <= WHOLE:
            return place
        return place.at[pl.ds(pl.multiple_of(way * (shard // 2), shard // 2), shard // 2)]

    def source(hop, way):
        return (z - (1 - 2 * way) * hop + 2 * DEPTH) % DEPTH

    def ring(way, hop, m):
        owner = source(hop - 1, way)
        place = spot(m, owner % HIGH, owner, hop, way)
        return remote(
            place, place, ring_s.at[way, hop - 1, m], ring_r.at[way, hop - 1, m],
            along(1 - 2 * way),
        )

    def ring_in(way, hop, m):
        owner = source(hop, way)
        place = spot(m, owner % HIGH, owner, hop, way)
        return remote(
            place, place, ring_s.at[way, hop - 1, m], ring_r.at[way, hop - 1, m],
            along(1 - 2 * way),
        )

    def own(m):
        place = weights[m].at[zl, zh, c]
        return remote(place, place, own_s.at[m], own_r.at[m], sibling)

    def sib(way, hop, m):
        owner = source(hop, way)
        place = spot(m, owner % HIGH, owner, hop, way)
        k = SHARED.index(hop)
        return remote(place, place, sib_s.at[way, k, m], sib_r.at[way, k, m], sibling)

    def edge_way(hop):
        return top if hop % 4 == 1 else 1 - top

    def edge(hop, m):
        way = edge_way(hop)
        owner = source(hop, way)
        src = spot(m, owner % HIGH, owner, hop, way)
        dst = spot(m, HIGH, owner, hop, way)
        column = (e + HIGH * (1 - 2 * top) + experts) % experts
        k = hop // 2
        return remote(src, dst, edge_s.at[k, m], edge_r.at[k, m], (column, t))

    def esib(hop, m):
        way = edge_way(hop)
        owner = source(hop, way)
        place = spot(m, HIGH, owner, hop, way)
        k = hop // 2
        return remote(place, place, esib_s.at[k, m], esib_r.at[k, m], sibling)

    def edge_arrive(hop):
        @pl.when(on_edge)
        def _():
            for m in range(3):
                edge(hop, m).wait_recv()
                esib(hop, m).start()

    def tick(hop):
        for m in range(3):
            for way in range(2):
                ring_in(way, hop, m).wait_recv()
                if hop < HOPS:
                    ring(way, hop + 1, m).start()
        if hop % 2 == 1:
            @pl.when(on_edge)
            def _():
                for m in range(3):
                    edge(hop, m).start()
        if hop in SHARED:
            for m in range(3):
                for way in range(2):
                    sib(way, hop, m).start()
        if hop % 2 == 1 and hop > 1:
            edge_arrive(hop - 2)

    for w, mine in zip(weights, (gate_in, up_in, down_in)):
        w[zl, zh, c] = mine[...]
    for m in range(3):
        for way in range(2):
            ring(way, 1, m).start()
    for m in range(3):
        own(m).start()

    targets_of = (None, along(1), along(-1), along(skip))
    sources_of = (None, along(-1), along(1), along(-skip))

    def line_x(b, i):
        return remote(xg.at[b, 0], xg.at[b, i], zx_s.at[b, i], zx_r.at[b, i], targets_of[i])

    def line_r(b, i):
        return remote(rg.at[b, 0], rg.at[b, i], zr_s.at[b, i], zr_r.at[b, i], targets_of[i])

    def part_out(b, i):
        return remote(part.at[b, i], precv.at[b, i], p_s.at[b, i], p_r.at[b, i], sources_of[i])

    scale = gain[...].astype(F32)
    for b, (x, r) in enumerate(((x1, r1), (x2, r2))):
        values = x[...].astype(F32)
        square = jnp.mean(values * values, axis=-1, keepdims=True)
        xg[b, 0] = (values * lax.rsqrt(square + EPS) * scale).astype(BF16)
        rg[b, 0] = r[...]
        for i in range(1, LINE):
            line_x(b, i).start()
            line_r(b, i).start()

    def block_send(b, d, src, dst, ss, rs, ls):
        @pl.when(d != p)
        def _():
            remote(
                src.at[b, d, pl.ds(0, ROWS)], dst.at[b, p, pl.ds(0, ROWS)],
                ss.at[b, d], rs.at[b, p], (d * HIGH + zl, t),
            ).start()

        @pl.when(d == p)
        def _():
            pltpu.make_async_copy(
                src.at[b, d, pl.ds(0, ROWS)], dst.at[b, p, pl.ds(0, ROWS)], ls.at[b]
            ).start()

    def group_send(b, q, src, dst, ss, rs, ls):
        for k in ORDER:
            block_send(b, q * WIDE + (py + k) % WIDE, src, dst, ss, rs, ls)

    def block_wait(b, src, dst, ss, rs, ls, which):
        def one(o, carry):
            d = (p + o) % PLANE
            copy = remote(
                src.at[b, d, pl.ds(0, ROWS)], dst.at[b, d, pl.ds(0, ROWS)],
                ss.at[b, d], rs.at[b, d], (d * HIGH + zl, t),
            )
            if which == "in":
                copy.wait_recv()
            else:
                copy.wait_send()
            return carry

        lax.fori_loop(1, PLANE, one, 0)
        if which == "in":
            pltpu.make_async_copy(
                src.at[b, p, pl.ds(0, ROWS)], dst.at[b, p, pl.ds(0, ROWS)], ls.at[b]
            ).wait()

    def route(b):
        ids = (lax.broadcasted_iota(jnp.int32, (PLANE, tokens), 0) * HIGH + zl).astype(F32)
        first = lax.broadcasted_iota(jnp.int32, (tokens, tokens), 0)
        second = lax.broadcasted_iota(jnp.int32, (tokens, tokens), 1)
        ahead = jnp.where(first < second, 1.0, 0.0).astype(BF16)
        targets, gates = [], []
        for i in range(LINE):
            info = rg[b, i]
            named = jnp.zeros((PLANE, tokens), F32)
            gate = jnp.zeros((PLANE, tokens), F32)
            for k in range(8):
                same = info[k:k + 1, :] == ids
                named = named + jnp.where(same, 1.0, 0.0)
                gate = gate + jnp.where(same, info[8 + k:9 + k, :], 0.0)
            rank = jnp.dot(named.astype(BF16), ahead, preferred_element_type=F32)
            targets.append(jnp.where(named > 0.5, rank * LINE + i, -1.0))
            gates.append(gate)
        tgt[b] = jnp.concatenate(targets, axis=1)
        gat[b] = jnp.concatenate(gates, axis=1)

    places = lax.broadcasted_iota(jnp.int32, (PAD, LINE * tokens), 0).astype(F32)

    def dispatch(b):
        for i in range(1, LINE):
            line_x(b, i).wait_recv()
            line_r(b, i).wait_recv()
        route(b)
        for d in range(PLANE):
            pick[d] = jnp.where(tgt[b, d:d + 1, :] == places, 1.0, 0.0).astype(BF16)
        for k in ORDER:
            q = (px + k) % WIDE
            rows = pick[pl.ds(q * WIDE, WIDE)].reshape(WIDE * PAD, LINE * tokens)
            block = jnp.dot(
                rows, xg[b].reshape(LINE * tokens, features), preferred_element_type=F32
            ).astype(BF16)
            outg[b, pl.ds(q * WIDE, WIDE)] = block.reshape(WIDE, PAD, features)
            group_send(b, q, outg, recv, a_s, a_r, a_l)

    def experts_on(b, v, k):
        q = (px + k) % WIDE
        rows = recv[b, pl.ds(q * WIDE, WIDE)].reshape(WIDE * PAD, features)
        gate_act = jnp.dot(rows, wg[v].reshape(features, inner), preferred_element_type=F32)
        up_act = jnp.dot(rows, wu[v].reshape(features, inner), preferred_element_type=F32)
        hidden = (gate_act / (1.0 + jnp.exp(-gate_act)) * up_act).astype(BF16)
        result = lax.dot_general(
            hidden, wd[v].reshape(features, inner), (((1,), (1,)), ((), ())),
            preferred_element_type=F32,
        ).astype(BF16)
        res[b, pl.ds(q * WIDE, WIDE)] = result.reshape(WIDE, PAD, features)
        group_send(b, q, res, back, b_s, b_r, b_l)

    def combine(b):
        for d in range(PLANE):
            pick[d] = jnp.where(
                tgt[b, d:d + 1, :] == places, gat[b, d:d + 1, :], 0.0
            ).astype(BF16)
        mixer = pick[...].reshape(PLANE * PAD, LINE * tokens)
        total = lax.dot_general(
            mixer, back[b].reshape(PLANE * PAD, features), (((0,), (0,)), ((), ())),
            preferred_element_type=F32,
        ).astype(BF16)
        part[b] = total.reshape(LINE, tokens, features)
        for i in range(1, LINE):
            part_out(b, i).start()

    def finish(b, out):
        total = part[b, 0].astype(F32)
        for i in range(1, LINE):
            part_out(b, i).wait_recv()
            total = total + precv[b, i].astype(F32)
        out[...] = total.astype(BF16)

    dispatch(0)
    tick(1)
    dispatch(1)
    for hop in range(2, 9):
        tick(hop)

    block_wait(0, outg, recv, a_s, a_r, a_l, "in")
    for m in range(3):
        own(m).wait_recv()
        for hop in (4, 8):
            for way in range(2):
                sib(way, hop, m).wait_recv()
    experts_on(0, zl, 2)
    experts_on(0, zl, 1)
    tick(9)
    experts_on(0, zl, 3)
    experts_on(0, zl, 0)
    tick(10)
    tick(11)
    block_wait(1, outg, recv, a_s, a_r, a_l, "in")
    edge_arrive(11)
    for m in range(3):
        for hop in SHARED:
            if hop not in (4, 8):
                for way in range(2):
                    sib(way, hop, m).wait_recv()

    @pl.when(on_edge)
    def _():
        for m in range(3):
            for hop in range(1, HOPS + 1, 2):
                esib(hop, m).wait_recv()

    wanted = tnew[e]
    keeps = wanted == told[e]
    lower = wanted == told[(e + experts - 1) % experts]
    bottom = 1 - (zl + HIGH - 1) // HIGH
    column = jnp.where(
        keeps, zl, jnp.where(lower, zl - 1 + bottom * (HIGH + 1), zl + 1)
    )
    for k in ORDER:
        experts_on(1, column, k)
    block_wait(0, res, back, b_s, b_r, b_l, "in")
    combine(0)
    block_wait(1, res, back, b_s, b_r, b_l, "in")
    combine(1)
    finish(0, o1)
    finish(1, o2)

    for m in range(3):
        own(m).wait_send()
        for way in range(2):
            for hop in range(1, HOPS + 1):
                ring(way, hop, m).wait_send()
            for hop in SHARED:
                sib(way, hop, m).wait_send()

    @pl.when(on_edge)
    def _():
        for m in range(3):
            for hop in range(1, HOPS + 1, 2):
                edge(hop, m).wait_send()
                esib(hop, m).wait_send()

    for b in range(2):
        for i in range(1, LINE):
            line_x(b, i).wait_send()
            line_r(b, i).wait_send()
            part_out(b, i).wait_send()
        block_wait(b, outg, recv, a_s, a_r, a_l, "out")
        block_wait(b, res, back, b_s, b_r, b_l, "out")


def local(
    batch_one, batch_two, norm_gain, slots_one, slots_two, gates_one, gates_two,
    table_old, table_new, gate_old, up_old, down_old,
):
    tokens, features = batch_one.shape
    shard, inner = gate_old.shape[1:]
    info = [
        jnp.concatenate([slots.astype(F32).T, gates.T], axis=0)
        for slots, gates in ((slots_one, gates_one), (slots_two, gates_two))
    ]
    vmem = pl.BlockSpec(memory_space=pltpu.VMEM)
    smem = pl.BlockSpec(memory_space=pltpu.SMEM)
    dma = pltpu.SemaphoreType.DMA
    full = pltpu.VMEM((HIGH + 1, HIGH, 2, shard, inner), BF16)
    blocks = pltpu.VMEM((2, PLANE, PAD, features), BF16)
    line = pltpu.VMEM((2, LINE, tokens, features), BF16)
    return pl.pallas_call(
        body,
        out_shape=[jax.ShapeDtypeStruct((tokens, features), BF16)] * 2,
        in_specs=[vmem] * 5 + [smem] * 2 + [vmem] * 3,
        out_specs=[vmem] * 2,
        scratch_shapes=[
            full, full, full,
            line, pltpu.VMEM((2, LINE, 16, tokens), F32),
            blocks, blocks, blocks, blocks,
            pltpu.VMEM((PLANE, PAD, LINE * tokens), BF16),
            line, line,
            pltpu.VMEM((2, PLANE, LINE * tokens), F32), pltpu.VMEM((2, PLANE, LINE * tokens), F32),
            dma((2, HOPS, 3)), dma((2, HOPS, 3)), dma((3,)), dma((3,)),
            dma((2, len(SHARED), 3)), dma((2, len(SHARED), 3)),
            dma((6, 3)), dma((6, 3)), dma((6, 3)), dma((6, 3)),
            dma((2, LINE)), dma((2, LINE)), dma((2, LINE)), dma((2, LINE)),
            dma((2, PLANE)), dma((2, PLANE)), dma((2,)),
            dma((2, PLANE)), dma((2, PLANE)), dma((2,)),
            dma((2, LINE)), dma((2, LINE)),
        ],
        compiler_params=pltpu.CompilerParams(
            collective_id=0, has_side_effects=True, vmem_limit_bytes=60 * 1024 * 1024
        ),
    )(
        batch_one, batch_two, norm_gain.reshape(1, features), info[0], info[1],
        table_old, table_new, gate_old[0], up_old[0], down_old[0].T,
    )


def solution(mesh):
    rows = P(("expert", "tensor"), None)
    in_specs = (
        rows, rows, P(), rows, rows, rows, rows, P(), P(),
        P("expert", "tensor", None), P("expert", "tensor", None), P("expert", None, "tensor"),
    )
    return jax.shard_map(
        local, mesh=mesh, in_specs=in_specs, out_specs=(rows, rows), check_vma=False
    )
```

time: 286 us -> 244 us (0.85)
  the two profiles are of different devices: /device:TPU:63 before, /device:TPU:1 now
where the time goes in v2:
time: 244 us; the launch traced here: 241 us
  Pallas kernels  235 us (96%)
  local copies, waits for them, and re-layouts  5.09 us (2%)
    pallas_call x1, Pallas kernels, local(): pl.pallas_call(body, out_shape=[jax.ShapeDtypeStruct((tokens, features),...  235 us

profile of v2, /device:TPU:1, one launch (start us, length us, event | category | flops | bytes accessed | tf_op | source)
XLA Modules:
  0.0 241.0 jit_solution(5115937041238065849)
XLA Ops:
  0.6 0.0 copy-start.1
  0.6 0.7 copy-done.1
  1.3 0.0 copy-start.2
  1.3 0.7 copy-done.2
  2.0 0.0 copy-start.3
  2.0 0.7 copy-done.3
  2.7 0.0 copy-start.4
  2.7 0.0 copy-start.5
  2.7 0.6 reshape.7.gain
  3.3 0.1 copy-done.4
  3.4 0.0 copy-done.5
  3.4 0.6 pad_maximum_fusion
  4.0 234.7 %shard_map.131 = (bf16[64,1536]{1,0:T(8,128)(2,1)}, bf16[64,1536]{1,0:T(8,128)(2,1)}) custom-call(bf16[64,1536]{1,0:T(8,128)(2,1)} %x1.1, bf16[64,1536]{1,0:T(8,128)(2,1)} %x2.1, bf16[1,1536]{1,0:T(2,128)(2,1)} %reshape.7.gain, f32[16,64]{1,0:T(8,128)} %get-tuple-element.2.r1, f32[16,64]{1,0:T(8,128)} %get-tuple-element.3.r2, s32[64]{0:T(128)} %told.1, ...), custom_call_target="tpu_custom_call" | custom-call | tf_op jit(solution)/shard_map/pallas_call | solution.py:390
  238.7 0.0 copy-start
  238.7 1.7 copy.16
  240.3 0.0 copy-done
  240.3 0.7 copy.17
  (2 shorter events, 0.0 us)
Async XLA Ops:
  0.6 0.7 copy-start.1
  1.3 0.7 copy-start.2
  2.0 0.7 copy-start.3
  2.7 0.7 copy-start.4
  2.7 0.7 copy-start.5
  238.7 1.7 copy-start

commit v3 on v2

--- a/solution.py
+++ b/solution.py
@@ -19,14 +19,16 @@
 WIDE = 4
 ROWS = 40
 PAD = 48
-HOPS = 11
 WHOLE = 4
-SHARED = (1, 3, 4, 5, 7, 8, 9, 11)
+HOPS = 9
+REST = 10
+SHARED = (1, 3, 4, 5, 7, 8, 9, REST)
+EDGES = (1, 3, 5, 7, 9, REST)
 ORDER = (2, 1, 3, 0)
 
 
 def body(
-    x1, x2, gain, r1, r2, told, tnew, gate_in, up_in, down_in,
+    x1, x2, gain, s1, s2, g1, g2, told, tnew, gate_in, up_in, down_in,
     o1, o2,
     wg, wu, wd, xg, rg, outg, recv, res, back, pick, part, precv, tgt, gat,
     ring_s, ring_r, own_s, own_r, sib_s, sib_r, edge_s, edge_r, esib_s, esib_r,
@@ -47,6 +49,7 @@
     skip = 2 * (1 - 2 * (z % 2))
     sibling = (e, zh * 2 + (1 - c))
     weights = (wg, wu, wd)
+    shards = (gate_in, up_in, down_in)
     tokens, features = x1.shape
     shard, inner = gate_in.shape
 
@@ -60,11 +63,6 @@
             device_id=device, device_id_type=MESH,
         )
 
-    blank = jnp.zeros((PLANE, 16, features), BF16)
-    for b in range(2):
-        recv[b, :, PAD - 16:PAD, :] = blank
-        back[b, :, PAD - 16:PAD, :] = blank
-
     barrier = pltpu.get_barrier_semaphore()
 
     def greet(device):
@@ -80,87 +78,94 @@
     lax.fori_loop(1, PLANE, greet_plane, 0)
     pl.semaphore_wait(barrier, 5 + PLANE - 1)
 
-    def spot(m, column, owner, hop, way):
+    def spot(m, column, owner, piece, way):
         place = weights[m].at[column, owner // HIGH, c]
-        if hop <= WHOLE:
+        if piece <= WHOLE:
             return place
-        return place.at[pl.ds(pl.multiple_of(way * (shard // 2), shard // 2), shard // 2)]
-
-    def source(hop, way):
-        return (z - (1 - 2 * way) * hop + 2 * DEPTH) % DEPTH
-
-    def ring(way, hop, m):
-        owner = source(hop - 1, way)
-        place = spot(m, owner % HIGH, owner, hop, way)
+        half = 1 - way if piece == REST else way
+        return place.at[pl.ds(pl.multiple_of(half * (shard // 2), shard // 2), shard // 2)]
+
+    def source(piece, way, back_off=0):
+        distance = (WHOLE + 1 if piece == REST else piece) - back_off
+        return (z - (1 - 2 * way) * distance + 2 * DEPTH) % DEPTH
+
+    def ring(way, piece, m):
+        owner = source(piece, way, 1)
+        place = spot(m, owner % HIGH, owner, piece, way)
         return remote(
-            place, place, ring_s.at[way, hop - 1, m], ring_r.at[way, hop - 1, m],
+            shards[m] if piece == 1 else place, place,
+            ring_s.at[way, piece - 1, m], ring_r.at[way, piece - 1, m], along(1 - 2 * way),
+        )
+
+    def ring_in(way, piece, m):
+        owner = source(piece, way)
+        place = spot(m, owner % HIGH, owner, piece, way)
+        return remote(
+            place, place, ring_s.at[way, piece - 1, m], ring_r.at[way, piece - 1, m],
             along(1 - 2 * way),
         )
 
-    def ring_in(way, hop, m):
-        owner = source(hop, way)
-        place = spot(m, owner % HIGH, owner, hop, way)
+    def own(m):
+        return remote(shards[m], weights[m].at[zl, zh, c], own_s.at[m], own_r.at[m], sibling)
+
+    def own_in(m):
         return remote(
-            place, place, ring_s.at[way, hop - 1, m], ring_r.at[way, hop - 1, m],
-            along(1 - 2 * way),
+            shards[m], weights[m].at[zl, zh, 1 - c], own_s.at[m], own_r.at[m], sibling
         )
 
-    def own(m):
-        place = weights[m].at[zl, zh, c]
-        return remote(place, place, own_s.at[m], own_r.at[m], sibling)
-
-    def sib(way, hop, m):
-        owner = source(hop, way)
-        place = spot(m, owner % HIGH, owner, hop, way)
-        k = SHARED.index(hop)
+    def sib(way, piece, m):
+        owner = source(piece, way)
+        place = spot(m, owner % HIGH, owner, piece, way)
+        k = SHARED.index(piece)
         return remote(place, place, sib_s.at[way, k, m], sib_r.at[way, k, m], sibling)
 
-    def edge_way(hop):
-        return top if hop % 4 == 1 else 1 - top
-
-    def edge(hop, m):
-        way = edge_way(hop)
-        owner = source(hop, way)
-        src = spot(m, owner % HIGH, owner, hop, way)
-        dst = spot(m, HIGH, owner, hop, way)
+    def edge_way(piece):
+        return 1 - top if piece % 4 == 3 else top
+
+    def edge(piece, m):
+        way = edge_way(piece)
+        owner = source(piece, way)
+        src = spot(m, owner % HIGH, owner, piece, way)
+        dst = spot(m, HIGH, owner, piece, way)
         column = (e + HIGH * (1 - 2 * top) + experts) % experts
-        k = hop // 2
+        k = EDGES.index(piece)
         return remote(src, dst, edge_s.at[k, m], edge_r.at[k, m], (column, t))
 
-    def esib(hop, m):
-        way = edge_way(hop)
-        owner = source(hop, way)
-        place = spot(m, HIGH, owner, hop, way)
-        k = hop // 2
+    def esib(piece, m):
+        way = edge_way(piece)
+        owner = source(piece, way)
+        place = spot(m, HIGH, owner, piece, way)
+        k = EDGES.index(piece)
         return remote(place, place, esib_s.at[k, m], esib_r.at[k, m], sibling)
 
-    def edge_arrive(hop):
+    def edge_arrive(*pieces):
         @pl.when(on_edge)
         def _():
-            for m in range(3):
-                edge(hop, m).wait_recv()
-                esib(hop, m).start()
-
-    def tick(hop):
+            for piece in pieces:
+                for m in range(3):
+                    edge(piece, m).wait_recv()
+                    esib(piece, m).start()
+
+    def tick(piece):
         for m in range(3):
             for way in range(2):
-                ring_in(way, hop, m).wait_recv()
-                if hop < HOPS:
-                    ring(way, hop + 1, m).start()
-        if hop % 2 == 1:
+                ring_in(way, piece, m).wait_recv()
+                if piece < HOPS:
+                    ring(way, piece + 1, m).start()
+        if piece == HOPS - 1:
+            for m in range(3):
+                for way in range(2):
+                    ring(way, REST, m).start()
+        if piece in EDGES:
             @pl.when(on_edge)
             def _():
                 for m in range(3):
-                    edge(hop, m).start()
-        if hop in SHARED:
+                    edge(piece, m).start()
+        if piece in SHARED:
             for m in range(3):
                 for way in range(2):
-                    sib(way, hop, m).start()
-        if hop % 2 == 1 and hop > 1:
-            edge_arrive(hop - 2)
-
-    for w, mine in zip(weights, (gate_in, up_in, down_in)):
-        w[zl, zh, c] = mine[...]
+                    sib(way, piece, m).start()
+
     for m in range(3):
         for way in range(2):
             ring(way, 1, m).start()
@@ -180,14 +185,23 @@
         return remote(part.at[b, i], precv.at[b, i], p_s.at[b, i], p_r.at[b, i], sources_of[i])
 
     scale = gain[...].astype(F32)
-    for b, (x, r) in enumerate(((x1, r1), (x2, r2))):
+    for b, (x, slots, gates) in enumerate(((x1, s1, g1), (x2, s2, g2))):
         values = x[...].astype(F32)
         square = jnp.mean(values * values, axis=-1, keepdims=True)
         xg[b, 0] = (values * lax.rsqrt(square + EPS) * scale).astype(BF16)
-        rg[b, 0] = r[...]
+        rg[b, 0, 0:8] = slots[...].astype(F32)
+        rg[b, 0, 8:16] = gates[...]
         for i in range(1, LINE):
             line_x(b, i).start()
             line_r(b, i).start()
+
+    for w, mine in zip(weights, shards):
+        w[zl, zh, c] = mine[...]
+
+    blank = jnp.zeros((PLANE, PAD - ROWS, features), BF16)
+    for b in range(2):
+        recv[b, :, ROWS:PAD, :] = blank
+        back[b, :, ROWS:PAD, :] = blank
 
     def block_send(b, d, src, dst, ss, rs, ls):
         @pl.when(d != p)
@@ -296,40 +310,42 @@
         for i in range(1, LINE):
             part_out(b, i).wait_recv()
             total = total + precv[b, i].astype(F32)
-        out[...] = total.astype(BF16)
+        out[...] = total
 
     dispatch(0)
     tick(1)
     dispatch(1)
-    for hop in range(2, 9):
-        tick(hop)
+    for piece in range(2, 7):
+        tick(piece)
+    edge_arrive(1)
+    tick(7)
+    tick(8)
 
     block_wait(0, outg, recv, a_s, a_r, a_l, "in")
     for m in range(3):
-        own(m).wait_recv()
-        for hop in (4, 8):
+        own_in(m).wait_recv()
+        for piece in (4, 8):
             for way in range(2):
-                sib(way, hop, m).wait_recv()
+                sib(way, piece, m).wait_recv()
     experts_on(0, zl, 2)
     experts_on(0, zl, 1)
     tick(9)
     experts_on(0, zl, 3)
+    tick(REST)
     experts_on(0, zl, 0)
-    tick(10)
-    tick(11)
     block_wait(1, outg, recv, a_s, a_r, a_l, "in")
-    edge_arrive(11)
+    edge_arrive(3, 5, 7, 9, REST)
     for m in range(3):
-        for hop in SHARED:
-            if hop not in (4, 8):
+        for piece in SHARED:
+            if piece not in (4, 8):
                 for way in range(2):
-                    sib(way, hop, m).wait_recv()
+                    sib(way, piece, m).wait_recv()
 
     @pl.when(on_edge)
     def _():
         for m in range(3):
-            for hop in range(1, HOPS + 1, 2):
-                esib(hop, m).wait_recv()
+            for piece in EDGES:
+                esib(piece, m).wait_recv()
 
     wanted = tnew[e]
     keeps = wanted == told[e]
@@ -350,17 +366,17 @@
     for m in range(3):
         own(m).wait_send()
         for way in range(2):
-            for hop in range(1, HOPS + 1):
-                ring(way, hop, m).wait_send()
-            for hop in SHARED:
-                sib(way, hop, m).wait_send()
+            for piece in range(1, REST + 1):
+                ring(way, piece, m).wait_send()
+            for piece in SHARED:
+                sib(way, piece, m).wait_send()
 
     @pl.when(on_edge)
     def _():
         for m in range(3):
-            for hop in range(1, HOPS + 1, 2):
-                edge(hop, m).wait_send()
-                esib(hop, m).wait_send()
+            for piece in EDGES:
+                edge(piece, m).wait_send()
+                esib(piece, m).wait_send()
 
     for b in range(2):
         for i in range(1, LINE):
@@ -377,20 +393,16 @@
 ):
     tokens, features = batch_one.shape
     shard, inner = gate_old.shape[1:]
-    info = [
-        jnp.concatenate([slots.astype(F32).T, gates.T], axis=0)
-        for slots, gates in ((slots_one, gates_one), (slots_two, gates_two))
-    ]
     vmem = pl.BlockSpec(memory_space=pltpu.VMEM)
     smem = pl.BlockSpec(memory_space=pltpu.SMEM)
     dma = pltpu.SemaphoreType.DMA
     full = pltpu.VMEM((HIGH + 1, HIGH, 2, shard, inner), BF16)
     blocks = pltpu.VMEM((2, PLANE, PAD, features), BF16)
     line = pltpu.VMEM((2, LINE, tokens, features), BF16)
-    return pl.pallas_call(
+    one, two = pl.pallas_call(
         body,
-        out_shape=[jax.ShapeDtypeStruct((tokens, features), BF16)] * 2,
-        in_specs=[vmem] * 5 + [smem] * 2 + [vmem] * 3,
+        out_shape=[jax.ShapeDtypeStruct((tokens, features), F32)] * 2,
+        in_specs=[vmem] * 7 + [smem] * 2 + [vmem] * 3,
         out_specs=[vmem] * 2,
         scratch_shapes=[
             full, full, full,
@@ -399,7 +411,7 @@
             pltpu.VMEM((PLANE, PAD, LINE * tokens), BF16),
             line, line,
             pltpu.VMEM((2, PLANE, LINE * tokens), F32), pltpu.VMEM((2, PLANE, LINE * tokens), F32),
-            dma((2, HOPS, 3)), dma((2, HOPS, 3)), dma((3,)), dma((3,)),
+            dma((2, REST, 3)), dma((2, REST, 3)), dma((3,)), dma((3,)),
             dma((2, len(SHARED), 3)), dma((2, len(SHARED), 3)),
             dma((6, 3)), dma((6, 3)), dma((6, 3)), dma((6, 3)),
             dma((2, LINE)), dma((2, LINE)), dma((2, LINE)), dma((2, LINE)),
@@ -411,9 +423,10 @@
             collective_id=0, has_side_effects=True, vmem_limit_bytes=60 * 1024 * 1024
         ),
     )(
-        batch_one, batch_two, norm_gain.reshape(1, features), info[0], info[1],
+        batch_one, batch_two, norm_gain, slots_one.T, slots_two.T, gates_one.T, gates_two.T,
         table_old, table_new, gate_old[0], up_old[0], down_old[0].T,
     )
+    return one.astype(BF16), two.astype(BF16)
 
 
 def solution(mesh):

time: 244 us -> 237 us (0.971)
  local copies, waits for them, and re-layouts: 5.09 us -> 0.01 us
  Pallas kernels: 235 us -> 232 us
    unnamed x14 -> x2, local copies, waits for them, and re-layouts: 4.49 us -> 0.01 us
    pallas_call x1, Pallas kernels: 235 us -> 232 us  [local(): pl.pallas_call(body, out_shape=[jax.ShapeDtypeStruct((tokens, features),...]
    convert_element_type x0 -> x2, other arithmetic: none -> 2.44 us  [local(): return (one.astype(BF16), two.astype(BF16))]
where the time goes in v3:
time: 237 us; the launch traced here: 235 us
  Pallas kernels  232 us (98%)
  other arithmetic  2.44 us (1%)
    pallas_call x1, Pallas kernels, local(): pl.pallas_call(body, out_shape=[jax.ShapeDtypeStruct((tokens, features),...  232 us

profile of v3, /device:TPU:1, one launch (start us, length us, event | category | flops | bytes accessed | tf_op | source)
XLA Modules:
  0.0 235.3 jit_solution(6726925352486782045)
XLA Ops:
  0.6 232.2 %shard_map.131 = (f32[64,1536]{1,0:T(8,128)}, f32[64,1536]{1,0:T(8,128)}) custom-call(bf16[64,1536]{1,0:T(8,128)(2,1)} %x1.1, bf16[64,1536]{1,0:T(8,128)(2,1)} %x2.1, bf16[1536]{0:T(1024)(128)(2,1)} %gain.1, s32[8,64]{1,0:T(8,128)} %bitcast.12, s32[8,64]{1,0:T(8,128)} %bitcast.13, f32[8,64]{1,0:T(8,128)} %bitcast.14, f32[8,64]{1,0:T(8,128)} %bitcast.15, ...), custom_call_target="tpu_custom_call" | custom-call | tf_op jit(solution)/shard_map/pallas_call | solution.py:402
  232.8 0.0 copy-start
  232.8 1.7 convert_element_type.6
  234.6 0.0 copy-done
  234.6 0.7 convert_element_type.7
Async XLA Ops:
  232.8 1.8 copy-start

commit v4 on v3

--- a/solution.py
+++ b/solution.py
@@ -25,6 +25,10 @@
 SHARED = (1, 3, 4, 5, 7, 8, 9, REST)
 EDGES = (1, 3, 5, 7, 9, REST)
 ORDER = (2, 1, 3, 0)
+FAR_FIRST = sorted(
+    ((dx, dy) for dx in range(WIDE) for dy in range(WIDE)),
+    key=lambda d: (-min(d[0], WIDE - d[0]) - min(d[1], WIDE - d[1]), d),
+)
 
 
 def body(
@@ -152,7 +156,7 @@
                 ring_in(way, piece, m).wait_recv()
                 if piece < HOPS:
                     ring(way, piece + 1, m).start()
-        if piece == HOPS - 1:
+        if piece == WHOLE:
             for m in range(3):
                 for way in range(2):
                     ring(way, REST, m).start()
@@ -289,7 +293,9 @@
             preferred_element_type=F32,
         ).astype(BF16)
         res[b, pl.ds(q * WIDE, WIDE)] = result.reshape(WIDE, PAD, features)
-        group_send(b, q, res, back, b_s, b_r, b_l)
+
+    def results_send(b, k):
+        group_send(b, (px + k) % WIDE, res, back, b_s, b_r, b_l)
 
     def combine(b):
         for d in range(PLANE):
@@ -315,10 +321,11 @@
     dispatch(0)
     tick(1)
     dispatch(1)
-    for piece in range(2, 7):
+    for piece in (2, 3, 4, 5, REST, 6):
         tick(piece)
     edge_arrive(1)
     tick(7)
+    edge_arrive(3)
     tick(8)
 
     block_wait(0, outg, recv, a_s, a_r, a_l, "in")
@@ -327,14 +334,13 @@
         for piece in (4, 8):
             for way in range(2):
                 sib(way, piece, m).wait_recv()
-    experts_on(0, zl, 2)
-    experts_on(0, zl, 1)
+    for k in ORDER:
+        experts_on(0, zl, k)
     tick(9)
-    experts_on(0, zl, 3)
-    tick(REST)
-    experts_on(0, zl, 0)
+    edge_arrive(5, REST, 7, 9)
+    for dx, dy in FAR_FIRST:
+        block_send(0, (px + dx) % WIDE * WIDE + (py + dy) % WIDE, res, back, b_s, b_r, b_l)
     block_wait(1, outg, recv, a_s, a_r, a_l, "in")
-    edge_arrive(3, 5, 7, 9, REST)
     for m in range(3):
         for piece in SHARED:
             if piece not in (4, 8):
@@ -356,6 +362,7 @@
     )
     for k in ORDER:
         experts_on(1, column, k)
+        results_send(1, k)
     block_wait(0, res, back, b_s, b_r, b_l, "in")
     combine(0)
     block_wait(1, res, back, b_s, b_r, b_l, "in")

time: 237 us -> 219 us (0.924)
  the two profiles are of different devices: /device:TPU:1 before, /device:TPU:56 now
where the time goes in v4:
time: 219 us
  Pallas kernels  216 us (99%)
  other arithmetic  2.44 us (1%)
    pallas_call x1, Pallas kernels, local(): pl.pallas_call(body, out_shape=[jax.ShapeDtypeStruct((tokens, features),...  216 us

profile of v4, /device:TPU:56, one launch (start us, length us, event | category | flops | bytes accessed | tf_op | source)
XLA Modules:
  0.0 218.6 jit_solution(124903266169555527)
XLA Ops:
  0.6 215.5 %shard_map.131 = (f32[64,1536]{1,0:T(8,128)}, f32[64,1536]{1,0:T(8,128)}) custom-call(bf16[64,1536]{1,0:T(8,128)(2,1)} %x1.1, bf16[64,1536]{1,0:T(8,128)(2,1)} %x2.1, bf16[1536]{0:T(1024)(128)(2,1)} %gain.1, s32[8,64]{1,0:T(8,128)} %bitcast.12, s32[8,64]{1,0:T(8,128)} %bitcast.13, f32[8,64]{1,0:T(8,128)} %bitcast.14, f32[8,64]{1,0:T(8,128)} %bitcast.15, ...), custom_call_target="tpu_custom_call" | custom-call | tf_op jit(solution)/shard_map/pallas_call | solution.py:409
  216.2 0.0 copy-start
  216.2 1.7 convert_element_type.6
  217.9 0.0 copy-done
  217.9 0.7 convert_element_type.7
Async XLA Ops:
  216.2 1.8 copy-start

commit v5 on v4

--- a/solution.py
+++ b/solution.py
@@ -33,7 +33,7 @@
 
 def body(
     x1, x2, gain, s1, s2, g1, g2, told, tnew, gate_in, up_in, down_in,
-    o1, o2,
+    out,
     wg, wu, wd, xg, rg, outg, recv, res, back, pick, part, precv, tgt, gat,
     ring_s, ring_r, own_s, own_r, sib_s, sib_r, edge_s, edge_r, esib_s, esib_r,
     zx_s, zx_r, zr_s, zr_r, a_s, a_r, a_l, b_s, b_r, b_l, p_s, p_r,
@@ -185,9 +185,6 @@
     def line_r(b, i):
         return remote(rg.at[b, 0], rg.at[b, i], zr_s.at[b, i], zr_r.at[b, i], targets_of[i])
 
-    def part_out(b, i):
-        return remote(part.at[b, i], precv.at[b, i], p_s.at[b, i], p_r.at[b, i], sources_of[i])
-
     scale = gain[...].astype(F32)
     for b, (x, slots, gates) in enumerate(((x1, s1, g1), (x2, s2, g2))):
         values = x[...].astype(F32)
@@ -207,30 +204,39 @@
         recv[b, :, ROWS:PAD, :] = blank
         back[b, :, ROWS:PAD, :] = blank
 
-    def block_send(b, d, src, dst, ss, rs, ls):
+    def rows_of(ref, b, d, cut):
+        if cut == 0:
+            return ref.at[b, d, pl.ds(0, ROWS)]
+        return ref.at[b, d, pl.ds(0, ROWS), pl.ds((cut - 1) * (features // 2), features // 2)]
+
+    def block_send(b, d, src, dst, ss, rs, ls, cut=0):
+        k = b + max(cut - 1, 0)
+
         @pl.when(d != p)
         def _():
             remote(
-                src.at[b, d, pl.ds(0, ROWS)], dst.at[b, p, pl.ds(0, ROWS)],
-                ss.at[b, d], rs.at[b, p], (d * HIGH + zl, t),
+                rows_of(src, b, d, cut), rows_of(dst, b, p, cut),
+                ss.at[k, d], rs.at[k, p], (d * HIGH + zl, t),
             ).start()
 
         @pl.when(d == p)
         def _():
             pltpu.make_async_copy(
-                src.at[b, d, pl.ds(0, ROWS)], dst.at[b, p, pl.ds(0, ROWS)], ls.at[b]
+                rows_of(src, b, d, cut), rows_of(dst, b, p, cut), ls.at[k]
             ).start()
 
     def group_send(b, q, src, dst, ss, rs, ls):
         for k in ORDER:
             block_send(b, q * WIDE + (py + k) % WIDE, src, dst, ss, rs, ls)
 
-    def block_wait(b, src, dst, ss, rs, ls, which):
+    def block_wait(b, src, dst, ss, rs, ls, which, cut=0):
+        k = b + max(cut - 1, 0)
+
         def one(o, carry):
             d = (p + o) % PLANE
             copy = remote(
-                src.at[b, d, pl.ds(0, ROWS)], dst.at[b, d, pl.ds(0, ROWS)],
-                ss.at[b, d], rs.at[b, d], (d * HIGH + zl, t),
+                rows_of(src, b, d, cut), rows_of(dst, b, d, cut),
+                ss.at[k, d], rs.at[k, d], (d * HIGH + zl, t),
             )
             if which == "in":
                 copy.wait_recv()
@@ -241,7 +247,7 @@
         lax.fori_loop(1, PLANE, one, 0)
         if which == "in":
             pltpu.make_async_copy(
-                src.at[b, p, pl.ds(0, ROWS)], dst.at[b, p, pl.ds(0, ROWS)], ls.at[b]
+                rows_of(src, b, p, cut), rows_of(dst, b, p, cut), ls.at[k]
             ).wait()
 
     def route(b):
@@ -294,29 +300,47 @@
         ).astype(BF16)
         res[b, pl.ds(q * WIDE, WIDE)] = result.reshape(WIDE, PAD, features)
 
-    def results_send(b, k):
-        group_send(b, (px + k) % WIDE, res, back, b_s, b_r, b_l)
-
-    def combine(b):
+    def results_send(b, cut):
+        for dx, dy in FAR_FIRST:
+            d = (px + dx) % WIDE * WIDE + (py + dy) % WIDE
+            block_send(b, d, res, back, b_s, b_r, b_l, cut)
+
+    def lanes(cut):
+        if cut == 0:
+            return pl.ds(0, features)
+        return pl.ds((cut - 1) * (features // 2), features // 2)
+
+    def part_out(b, i, cut):
+        k = b + max(cut - 1, 0)
+        return remote(
+            part.at[b, i, :, lanes(cut)], precv.at[b, i, :, lanes(cut)],
+            p_s.at[k, i], p_r.at[k, i], sources_of[i],
+        )
+
+    def weigh(b):
         for d in range(PLANE):
             pick[d] = jnp.where(
                 tgt[b, d:d + 1, :] == places, gat[b, d:d + 1, :], 0.0
             ).astype(BF16)
+
+    def combine(b, cut):
         mixer = pick[...].reshape(PLANE * PAD, LINE * tokens)
+        results = back[b, :, :, lanes(cut)]
+        width = results.shape[2]
         total = lax.dot_general(
-            mixer, back[b].reshape(PLANE * PAD, features), (((0,), (0,)), ((), ())),
+            mixer, results.reshape(PLANE * PAD, width), (((0,), (0,)), ((), ())),
             preferred_element_type=F32,
         ).astype(BF16)
-        part[b] = total.reshape(LINE, tokens, features)
-        for i in range(1, LINE):
-            part_out(b, i).start()
-
-    def finish(b, out):
-        total = part[b, 0].astype(F32)
-        for i in range(1, LINE):
-            part_out(b, i).wait_recv()
-            total = total + precv[b, i].astype(F32)
-        out[...] = total
+        part[b, :, :, lanes(cut)] = total.reshape(LINE, tokens, width)
+        for i in range(1, LINE):
+            part_out(b, i, cut).start()
+
+    def finish(b, cut):
+        total = part[b, 0, :, lanes(cut)].astype(F32)
+        for i in range(1, LINE):
+            part_out(b, i, cut).wait_recv()
+            total = total + precv[b, i, :, lanes(cut)].astype(F32)
+        out[b, :, lanes(cut)] = total
 
     dispatch(0)
     tick(1)
@@ -338,8 +362,7 @@
         experts_on(0, zl, k)
     tick(9)
     edge_arrive(5, REST, 7, 9)
-    for dx, dy in FAR_FIRST:
-        block_send(0, (px + dx) % WIDE * WIDE + (py + dy) % WIDE, res, back, b_s, b_r, b_l)
+    results_send(0, 0)
     block_wait(1, outg, recv, a_s, a_r, a_l, "in")
     for m in range(3):
         for piece in SHARED:
@@ -362,13 +385,18 @@
     )
     for k in ORDER:
         experts_on(1, column, k)
-        results_send(1, k)
+    for cut in (1, 2):
+        results_send(1, cut)
+    weigh(0)
     block_wait(0, res, back, b_s, b_r, b_l, "in")
-    combine(0)
-    block_wait(1, res, back, b_s, b_r, b_l, "in")
-    combine(1)
-    finish(0, o1)
-    finish(1, o2)
+    combine(0, 0)
+    weigh(1)
+    for cut in (1, 2):
+        block_wait(1, res, back, b_s, b_r, b_l, "in", cut)
+        combine(1, cut)
+    finish(0, 0)
+    for cut in (1, 2):
+        finish(1, cut)
 
     for m in range(3):
         own(m).wait_send()
@@ -389,9 +417,11 @@
         for i in range(1, LINE):
             line_x(b, i).wait_send()
             line_r(b, i).wait_send()
-            part_out(b, i).wait_send()
         block_wait(b, outg, recv, a_s, a_r, a_l, "out")
-        block_wait(b, res, back, b_s, b_r, b_l, "out")
+    for b, cut in ((0, 0), (1, 1), (1, 2)):
+        for i in range(1, LINE):
+            part_out(b, i, cut).wait_send()
+        block_wait(b, res, back, b_s, b_r, b_l, "out", cut)
 
 
 def local(
@@ -406,11 +436,11 @@
     full = pltpu.VMEM((HIGH + 1, HIGH, 2, shard, inner), BF16)
     blocks = pltpu.VMEM((2, PLANE, PAD, features), BF16)
     line = pltpu.VMEM((2, LINE, tokens, features), BF16)
-    one, two = pl.pallas_call(
+    mixed = pl.pallas_call(
         body,
-        out_shape=[jax.ShapeDtypeStruct((tokens, features), F32)] * 2,
+        out_shape=jax.ShapeDtypeStruct((2, tokens, features), F32),
         in_specs=[vmem] * 7 + [smem] * 2 + [vmem] * 3,
-        out_specs=[vmem] * 2,
+        out_specs=vmem,
         scratch_shapes=[
             full, full, full,
             line, pltpu.VMEM((2, LINE, 16, tokens), F32),
@@ -423,8 +453,8 @@
             dma((6, 3)), dma((6, 3)), dma((6, 3)), dma((6, 3)),
             dma((2, LINE)), dma((2, LINE)), dma((2, LINE)), dma((2, LINE)),
             dma((2, PLANE)), dma((2, PLANE)), dma((2,)),
-            dma((2, PLANE)), dma((2, PLANE)), dma((2,)),
-            dma((2, LINE)), dma((2, LINE)),
+            dma((3, PLANE)), dma((3, PLANE)), dma((3,)),
+            dma((3, LINE)), dma((3, LINE)),
         ],
         compiler_params=pltpu.CompilerParams(
             collective_id=0, has_side_effects=True, vmem_limit_bytes=60 * 1024 * 1024
@@ -433,7 +463,7 @@
         batch_one, batch_two, norm_gain, slots_one.T, slots_two.T, gates_one.T, gates_two.T,
         table_old, table_new, gate_old[0], up_old[0], down_old[0].T,
     )
-    return one.astype(BF16), two.astype(BF16)
+    return mixed[0].astype(BF16), mixed[1].astype(BF16)
 
 
 def solution(mesh):

time: 219 us -> 214 us (0.977)
  the two profiles are of different devices: /device:TPU:56 before, /device:TPU:1 now
where the time goes in v5:
time: 214 us; the launch traced here: 211 us
  Pallas kernels  208 us (97%)
    pallas_call x1, Pallas kernels, local(): pl.pallas_call(body, out_shape=jax.ShapeDtypeStruct((2, tokens, features)...  208 us

profile of v5, /device:TPU:1, one launch (start us, length us, event | category | flops | bytes accessed | tf_op | source)
XLA Modules:
  0.0 210.6 jit_solution(2289035922174817764)
XLA Ops:
  0.6 208.0 %shard_map.131 = f32[2,64,1536]{2,1,0:T(8,128)} custom-call(bf16[64,1536]{1,0:T(8,128)(2,1)} %x1.1, bf16[64,1536]{1,0:T(8,128)(2,1)} %x2.1, bf16[1536]{0:T(1024)(128)(2,1)} %gain.1, s32[8,64]{1,0:T(8,128)} %bitcast.16, s32[8,64]{1,0:T(8,128)} %bitcast.17, f32[8,64]{1,0:T(8,128)} %bitcast.18, f32[8,64]{1,0:T(8,128)} %bitcast.19, s32[64]{0:T(128)} %told.1, ...), custom_call_target="tpu_custom_call" | custom-call | tf_op jit(solution)/shard_map/pallas_call | solution.py:439
  208.7 1.2 convert.4
  209.8 0.8 slice_bitcast_fusion

commit v6 on v5

--- a/solution.py
+++ b/solution.py
@@ -343,8 +343,8 @@
         out[b, :, lanes(cut)] = total
 
     dispatch(0)
+    dispatch(1)
     tick(1)
-    dispatch(1)
     for piece in (2, 3, 4, 5, REST, 6):
         tick(piece)
     edge_arrive(1)

time: 214 us -> 205 us (0.958)
  Pallas kernels: 208 us -> 199 us
    pallas_call x1, Pallas kernels: 208 us -> 199 us  [local(): pl.pallas_call(body, out_shape=jax.ShapeDtypeStruct((2, tokens, features)...]
where the time goes in v6:
time: 205 us; the launch traced here: 202 us
  Pallas kernels  199 us (97%)
    pallas_call x1, Pallas kernels, local(): pl.pallas_call(body, out_shape=jax.ShapeDtypeStruct((2, tokens, features)...  199 us

profile of v6, /device:TPU:1, one launch (start us, length us, event | category | flops | bytes accessed | tf_op | source)
XLA Modules:
  0.0 201.7 jit_solution(11393000816113111792)
XLA Ops:
  0.6 199.1 %shard_map.131 = f32[2,64,1536]{2,1,0:T(8,128)} custom-call(bf16[64,1536]{1,0:T(8,128)(2,1)} %x1.1, bf16[64,1536]{1,0:T(8,128)(2,1)} %x2.1, bf16[1536]{0:T(1024)(128)(2,1)} %gain.1, s32[8,64]{1,0:T(8,128)} %bitcast.16, s32[8,64]{1,0:T(8,128)} %bitcast.17, f32[8,64]{1,0:T(8,128)} %bitcast.18, f32[8,64]{1,0:T(8,128)} %bitcast.19, s32[64]{0:T(128)} %told.1, ...), custom_call_target="tpu_custom_call" | custom-call | tf_op jit(solution)/shard_map/pallas_call | solution.py:439
  199.7 1.2 convert.4
  200.9 0.8 slice_bitcast_fusion
